TPU v7x, 32 devices: a whole 2x2x4 slice. The times are simulated.
32 devices in a mesh: frames: 8 (over z, x), heads: 4 (over y, core).
Axes of the slice: x: 2, y: 2, z: 4, core: 2. Of those that a mesh axis runs over, the one named last changes fastest.
Arguments:
- queries: bfloat16 [1024, 4096], P('frames', 'heads'), may hold values from -9 to 9
- keys: bfloat16 [1024, 512], P(('frames', 'heads')), may hold values from -4.5 to 4.5
- values: bfloat16 [1024, 512], P(('frames', 'heads')), may hold values from -6 to 6
- block_mask: int32 [8, 8], replicated, may hold values from 0 to 1, as said below
- lengths: int32 [8], replicated, may hold values from 64 to 128, as said below
Outputs:
- attended: bfloat16 [1024, 4096], P('frames', 'heads')
Inputs may be any that keep to these rules, and one draw needn't show every extreme that they name: block_mask[i, i] = 1 and block_mask[i, j] = 0 for j > i. `lengths`: some frame group is full in every draw.
All inputs are finite; a program needn't handle non-finite values.
Results may differ from a plain program's by a relative error of at most 0.0055.
Values may be sent and summed in bfloat16 or wider, within the bound.
A program may use at most 64 MiB of HBM per device.

v0:
```python
import math
import jax
import jax.numpy as jnp
from jax import lax
from jax.sharding import PartitionSpec as P

HEAD_DIM = 128
masked_score = -1e30


def attend(query_sets, keys_mine, values_mine, block_mask, lengths, group_tokens):
    kv_local = keys_mine.shape[1] // HEAD_DIM
    q_local = query_sets[0][0].shape[1] // HEAD_DIM
    per_kv = q_local // kv_local
    scale = HEAD_DIM ** (-0.5)
    group_count = block_mask.shape[0]
    group_ids = jnp.arange(group_count, dtype=jnp.int32)
    prepared = []
    initial = []
    for rows, owner in query_sets:
        count = rows.shape[0]
        prepared.append(
            (
                rows.reshape(count, kv_local, per_kv, HEAD_DIM),
                lax.dynamic_slice_in_dim(block_mask, owner, 1, 0)[0],
            )
        )
        initial.append(
            (
                jnp.full((kv_local, per_kv, count), masked_score, jnp.float32),
                jnp.zeros((kv_local, per_kv, count), jnp.float32),
                jnp.zeros((count, kv_local, per_kv, HEAD_DIM), jnp.float32),
            )
        )
    key_piece = lax.all_gather(keys_mine, "frames", axis=0, tiled=True)
    value_piece = lax.all_gather(values_mine, "frames", axis=0, tiled=True)
    fold_rows = key_piece.shape[0]
    width = math.gcd(fold_rows, 512)
    blocks = fold_rows // width
    key_blocks = key_piece.reshape(blocks, width, kv_local, HEAD_DIM)
    value_blocks = value_piece.reshape(blocks, width, kv_local, HEAD_DIM)

    def one_block(state, inputs):
        key_block, value_block, number = inputs
        positions = number * width + jnp.arange(width, dtype=jnp.int32)
        key_group = positions // group_tokens
        within = positions % group_tokens
        onehot = (key_group[:, None] == group_ids[None, :]).astype(jnp.int32)
        live_len = jnp.sum(onehot * lengths[None, :], axis=1)
        updated = []
        for (query_rows, mask_row), (running_max, running_total, running_acc) in zip(
            prepared, state
        ):
            allowed = jnp.sum(onehot * mask_row[None, :], axis=1)
            valid = (allowed > 0) & (within < live_len)

            def update(current):
                old_max, old_total, old_acc = current
                scores = (
                    jnp.einsum(
                        "tkgd,skd->kgts", query_rows, key_block, preferred_element_type=jnp.float32
                    )
                    * scale
                )
                scores = jnp.where(valid[None, None, None, :], scores, masked_score)
                new_max = jnp.maximum(old_max, jnp.max(scores, axis=-1))
                probs = jnp.exp(scores - new_max[..., None])
                factor = jnp.exp(old_max - new_max)
                new_total = old_total * factor + jnp.sum(probs, axis=-1)
                added = jnp.einsum(
                    "kgts,skd->tkgd",
                    probs.astype(jnp.bfloat16),
                    value_block,
                    preferred_element_type=jnp.float32,
                )
                new_acc = old_acc * jnp.transpose(factor, (2, 0, 1))[..., None] + added
                return (new_max, new_total, new_acc)

            updated.append(
                lax.cond(
                    jnp.any(valid),
                    update,
                    lambda current: current,
                    (running_max, running_total, running_acc),
                )
            )
        return (tuple(updated), None)

    numbers = jnp.arange(blocks, dtype=jnp.int32)
    final, unused = lax.scan(one_block, tuple(initial), (key_blocks, value_blocks, numbers))
    results = []
    for (rows, owner), (running_max, running_total, running_acc) in zip(query_sets, final):
        output = running_acc / jnp.transpose(running_total, (2, 0, 1))[..., None]
        results.append(output.astype(jnp.bfloat16).reshape(rows.shape[0], q_local * HEAD_DIM))
    return results


def local(queries, keys, values, block_mask, lengths):
    keys_mine, values_mine = (
        lax.all_to_all(keys, "heads", split_axis=1, concat_axis=0, tiled=True),
        lax.all_to_all(values, "heads", split_axis=1, concat_axis=0, tiled=True),
    )
    group_tokens = queries.shape[0]
    frame_index = lax.axis_index("frames")
    outputs = attend(
        [(queries, frame_index)], keys_mine, values_mine, block_mask, lengths, group_tokens
    )
    return outputs[0]


def solution(mesh):
    return jax.shard_map(
        local,
        mesh=mesh,
        in_specs=(
            P("frames", "heads"),
            P(("frames", "heads"), None),
            P(("frames", "heads"), None),
            P(),
            P(),
        ),
        out_specs=P("frames", "heads"),
        check_vma=False,
    )
```

profile of v0, /device:TPU:30, one launch (start us, length us, event | category | flops | bytes accessed | tf_op | source)
XLA Modules:
  0.0 84.3 jit_solution(984634713009666700)
XLA Ops:
  0.0 0.0 copy-start
  0.0 0.8 copy-done
  0.8 0.0 copy-start.1
  0.8 0.6 copy_bitcast_fusion
  1.4 3.7 %all-to-all-start.1 = ((bf16[32,4,128]{2,0,1:T(8,128)(2,1)}), bf16[32,4,128]{2,0,1:T(8,128)(2,1)S(1)}, u32[]{:S(2)}, u32[]{:S(2)}) async-start(bf16[32,4,128]{2,0,1:T(8,128)(2,1)} %copy_bitcast_fusion), calls=%async_computation.1 | async-start | bytes 65536 | tf_op jit(solution)/shard_map/all_to_all | solution.py:101
  5.1 1.4 %copy_bitcast_fusion.1 = bf16[32,4,128]{2,0,1:T(8,128)(2,1)} fusion(bf16[32,512]{1,0:T(8,128)(2,1)} %param.10), kind=kLoop, calls=%fused_computation.47 | loop fusion | bytes 65536 | tf_op jit(solution)/shard_map/all_to_all | solution.py:100
  6.5 0.7 constant_dynamic-slice_fusion
  7.2 1.1 %copy.37 = bf16[128,1024]{0,1:T(8,128)(2,1)S(1)} copy(bf16[128,1024]{1,0:T(8,128)(2,1)} %param.9) | data formatting | bytes 524288 | tf_op args[0]
  8.3 0.2 copy.39
  8.5 0.0 all-to-all-done.1
  8.5 3.8 %all-to-all-start = ((bf16[32,4,128]{2,0,1:T(8,128)(2,1)}), bf16[32,4,128]{2,0,1:T(8,128)(2,1)S(1)}, u32[]{:S(2)}, u32[]{:S(2)}) async-start(bf16[32,4,128]{2,0,1:T(8,128)(2,1)} %copy_bitcast_fusion.1), calls=%async_computation | async-start | bytes 65536 | tf_op jit(solution)/shard_map/all_to_all | solution.py:100
  12.3 30.8 %all_gather.7 = bf16[1024,128]{1,0:T(8,128)(2,1)S(1)} all-gather(bf16[128,128]{1,0:T(8,128)(2,1)S(1)} %bitcast.97), channel_id=1, replica_groups=mesh['frames'=8,'heads'=4] {'frames'}, dimensions={0}, use_global_device_ids=true | all-gather | bytes 294912 | tf_op jit(solution)/shard_map/all_gather | solution.py:36
  43.1 0.1 copy.40
  43.3 0.0 all-to-all-done
  43.3 30.7 %all_gather.6 = bf16[1024,128]{1,0:T(8,128)(2,1)S(1)} all-gather(bf16[128,128]{1,0:T(8,128)(2,1)S(1)} %bitcast.98), channel_id=1, replica_groups=mesh['frames'=8,'heads'=4] {'frames'}, dimensions={0}, use_global_device_ids=true | all-gather | bytes 294912 | tf_op jit(solution)/shard_map/all_gather | solution.py:35
  74.1 0.0 copy-done.1
  74.1 9.3 %while.17 = (s32[]{:T(128)}, f32[1,8,128]{2,1,0:T(8,128)S(1)}, f32[1,8,128]{2,1,0:T(8,128)S(1)}, f32[128,1,8,128]{0,3,2,1:T(8,128)S(1)}, s32[2]{0:T(128)S(1)}, /...) while((s32[]{:T(128)}, f32[1,8,128]{2,1,0:T(8,128)S(1)}, ...), condition=%wide.region_8.9_spmd.clone, body=%wide.region_0.8_spmd.clone.sunk | while | flops 274503680 | bytes 7944539 | solution.py:90
  74.1 0.6 dynamic_slice.43
  75.3 0.1 fusion.38
  75.4 0.7 fusion.39
  76.9 1.9 %conditional.3 = ((f32[1,8,128]{2,1,0:T(8,128)S(1)}, f32[1,8,128]{2,1,0:T(8,128)S(1)}, f32[128,1,8,128]{0,3,2,1:T(8,128)S(1)})) conditional(s32[]{:T(128)} %convert_element_type.23, (f32[1,8,128]{2,1,0:T(8,128)S(1)}, f32[1,8,128]{2,1,0:T(8,128)S(1)}, f32[128,1,8,128]{0,3,2,1:T(8,128)S(1)}) %tuple.59, (pred[512]{0:T(512)(128)(4,1)S(1)}, ...), branch_computations={%region_4.4_spmd, %region_5.7_spmd} | conditional | flops 274467840 | bytes 7931432 | solution.py:80
  76.9 0.5 bitcast_reduce_fusion
  77.4 0.8 fusion.5
  78.2 0.5 fusion.4
  78.7 0.6 dynamic_slice.43
  80.0 0.1 fusion.38
  80.1 0.7 fusion.39
  81.5 1.9 %conditional.3 = ((f32[1,8,128]{2,1,0:T(8,128)S(1)}, f32[1,8,128]{2,1,0:T(8,128)S(1)}, f32[128,1,8,128]{0,3,2,1:T(8,128)S(1)})) conditional(s32[]{:T(128)} %convert_element_type.23, (f32[1,8,128]{2,1,0:T(8,128)S(1)}, f32[1,8,128]{2,1,0:T(8,128)S(1)}, f32[128,1,8,128]{0,3,2,1:T(8,128)S(1)}) %tuple.59, (pred[512]{0:T(512)(128)(4,1)S(1)}, ...), branch_computations={%region_4.4_spmd, %region_5.7_spmd} | conditional | flops 274467840 | bytes 7931432 | solution.py:80
  81.5 0.5 bitcast_reduce_fusion
  82.0 0.8 fusion.5
  82.9 0.5 fusion.4
  83.4 0.1 divide_convert_fusion
  83.5 0.9 %copy.43 = bf16[128,1024]{1,0:T(8,128)(2,1)} copy(bf16[128,1024]{0,1:T(8,128)(2,1)S(1)} %bitcast.93) | data formatting | bytes 524288 | tf_op jit(solution)/shard_map/reshape | solution.py:94
  (12 shorter events, 0.1 us)
Async XLA Ops:
  0.0 0.8 copy-start
  0.8 73.3 %copy-start.1 = (s32[8]{0:T(128)S(1)}, s32[8]{0:T(128)}, u32[]{:S(2)}) copy-start(s32[8]{0:T(128)} %param.13) | copy-start | bytes 100
  1.4 7.1 %all-to-all-start.1 = ((bf16[32,4,128]{2,0,1:T(8,128)(2,1)}), bf16[32,4,128]{2,0,1:T(8,128)(2,1)S(1)}, u32[]{:S(2)}, u32[]{:S(2)}) async-start(bf16[32,4,128]{2,0,1:T(8,128)(2,1)} %copy_bitcast_fusion), calls=%async_computation.1 | async-start | bytes 65536 | tf_op jit(solution)/shard_map/all_to_all | solution.py:101
  8.5 34.8 %all-to-all-start = ((bf16[32,4,128]{2,0,1:T(8,128)(2,1)}), bf16[32,4,128]{2,0,1:T(8,128)(2,1)S(1)}, u32[]{:S(2)}, u32[]{:S(2)}) async-start(bf16[32,4,128]{2,0,1:T(8,128)(2,1)} %copy_bitcast_fusion.1), calls=%async_computation | async-start | bytes 65536 | tf_op jit(solution)/shard_map/all_to_all | solution.py:100
where the time goes:
time: 84.8 us; the launch traced here: 84.3 us
  blocking collectives  61.6 us (73%)
  starting transfers between devices  7.53 us (9%)
  local copies, waits for them, and re-layouts  6.95 us (8%)
  loops' own time  2.87 us (3%)
  other arithmetic  2.72 us (3%)
  matrix products  2.59 us (3%)
    all_gather x1, blocking collectives, attend(): value_piece = lax.all_gather(values_mine, 'frames', axis=0, tiled=True)  30.8 us
    all_gather x1, blocking collectives, attend(): key_piece = lax.all_gather(keys_mine, 'frames', axis=0, tiled=True)  30.7 us
    all_to_all x1, starting transfers between devices, local(): lax.all_to_all(keys, 'heads', split_axis=1, concat_axis=0, tiled=True)  3.79 us
    all_to_all x1, starting transfers between devices, local(): lax.all_to_all(values, 'heads', split_axis=1, concat_axis=0, tiled=True)  3.74 us
    another operation x1, loops' own time, attend(): lax.scan(one_block, tuple(initial), (key_blocks, value_blocks, numbers))  2.76 us
    unnamed x7, local copies, waits for them, and re-layouts  2.2 us
  transfers between devices with their start and end apart: 2, of which 0 were waited for; matrix products, arithmetic and copies ran while one was open for 4% of the time, Pallas kernels for 0%

commit v1 on v0

--- a/solution.py
+++ b/solution.py
@@ -97,7 +97,12 @@
 
 def local(queries, keys, values, block_mask, lengths):
     keys_mine, values_mine = (
-        lax.all_to_all(keys, "heads", split_axis=1, concat_axis=0, tiled=True),
+        jnp.concatenate(
+            lax.all_to_all(
+                jnp.stack(jnp.split(keys, lax.axis_size("heads"), axis=1)), "heads", 0, 0
+            ),
+            axis=0,
+        ),
         lax.all_to_all(values, "heads", split_axis=1, concat_axis=0, tiled=True),
     )
     group_tokens = queries.shape[0]

time: 84.8 us -> 84.3 us (level)
  local copies, waits for them, and re-layouts: 6.95 us -> 5.59 us
    all_to_all x1 -> x0, local copies, waits for them, and re-layouts: 1.38 us -> none  [local(): lax.all_to_all(keys, 'heads', split_axis=1, concat_axis=0, tiled=True)]
  transfers between devices with their start and end apart: 2 -> 2, of which waited for: 0 -> 0; matrix products, arithmetic and copies ran while one was open for 4% -> 3% of each run, Pallas kernels for 0% -> 0%
where the time goes in v1:
time: 84.3 us; the launch traced here: 83.9 us
  blocking collectives  61.6 us (73%)
  starting transfers between devices  8.28 us (10%)
  local copies, waits for them, and re-layouts  5.59 us (7%)
  other arithmetic  3.17 us (4%)
  loops' own time  2.61 us (3%)
  matrix products  2.59 us (3%)
    all_gather x1, blocking collectives, attend(): key_piece = lax.all_gather(keys_mine, 'frames', axis=0, tiled=True)  30.8 us
    all_gather x1, blocking collectives, attend(): value_piece = lax.all_gather(values_mine, 'frames', axis=0, tiled=True)  30.7 us
    all_to_all x1, starting transfers between devices, local(): lax.all_to_all(values, 'heads', split_axis=1, concat_axis=0, tiled=True)  4.54 us
    all_to_all x1, starting transfers between devices, local(): lax.all_to_all(jnp.stack(jnp.split(keys, lax.axis_size('heads'), axis=1))...  3.74 us
    another operation x1, loops' own time, attend(): lax.scan(one_block, tuple(initial), (key_blocks, value_blocks, numbers))  2.5 us
  transfers between devices with their start and end apart: 2, of which 0 were waited for; matrix products, arithmetic and copies ran while one was open for 3% of the time, Pallas kernels for 0%

profile of v1, /device:TPU:30, one launch (start us, length us, event | category | flops | bytes accessed | tf_op | source)
XLA Modules:
  0.0 83.9 jit_solution(12553481389251819885)
XLA Ops:
  0.0 0.0 copy-start
  0.0 0.0 copy-start.1
  0.0 0.8 slice_bitcast_fusion.3
  0.8 0.6 pad_maximum_fusion
  1.4 3.7 %all-to-all-start = ((bf16[4,32,128]{2,1,0:T(8,128)(2,1)}), bf16[4,32,128]{2,1,0:T(8,128)(2,1)S(1)}, u32[]{:S(2)}, u32[]{:S(2)}) async-start(bf16[4,32,128]{2,1,0:T(8,128)(2,1)} %pad_maximum_fusion), calls=%async_computation | async-start | bytes 65536 | tf_op jit(solution)/shard_map/all_to_all | solution.py:101
  5.1 0.0 copy-done
  5.1 0.6 copy_bitcast_fusion
  5.8 0.7 constant_dynamic-slice_fusion
  6.4 1.1 %copy.26 = bf16[128,1024]{0,1:T(8,128)(2,1)S(1)} copy(bf16[128,1024]{1,0:T(8,128)(2,1)} %param.9) | data formatting | bytes 524288 | tf_op args[0]
  7.6 0.2 copy.28
  7.8 0.0 all-to-all-done
  7.8 4.5 %all-to-all-start.1 = ((bf16[32,4,128]{2,0,1:T(8,128)(2,1)}), bf16[32,4,128]{2,0,1:T(8,128)(2,1)S(1)}, u32[]{:S(2)}, u32[]{:S(2)}) async-start(bf16[32,4,128]{2,0,1:T(8,128)(2,1)} %copy_bitcast_fusion), calls=%async_computation.1 | async-start | bytes 65536 | tf_op jit(solution)/shard_map/all_to_all | solution.py:106
  12.3 30.8 %all_gather.6 = bf16[1024,128]{1,0:T(8,128)(2,1)S(1)} all-gather(bf16[128,128]{1,0:T(8,128)(2,1)S(1)} %bitcast.98), channel_id=1, replica_groups=mesh['frames'=8,'heads'=4] {'frames'}, dimensions={0}, use_global_device_ids=true | all-gather | bytes 294912 | tf_op jit(solution)/shard_map/all_gather | solution.py:35
  43.1 0.0 all-to-all-done.1
  43.1 30.7 %all_gather.7 = bf16[1024,128]{1,0:T(8,128)(2,1)S(1)} all-gather(bf16[128,128]{1,0:T(8,128)(2,1)S(1)} %bitcast.99), channel_id=1, replica_groups=mesh['frames'=8,'heads'=4] {'frames'}, dimensions={0}, use_global_device_ids=true | all-gather | bytes 294912 | tf_op jit(solution)/shard_map/all_gather | solution.py:36
  73.9 0.1 copy.29
  74.1 0.0 copy-done.1
  74.1 8.9 %while.17 = (s32[]{:T(128)}, f32[1,8,128]{2,1,0:T(8,128)S(1)}, f32[1,8,128]{2,1,0:T(8,128)S(1)}, f32[128,1,8,128]{0,3,2,1:T(8,128)S(1)}, s32[2]{0:T(128)S(1)}, /...) while((s32[]{:T(128)}, f32[1,8,128]{2,1,0:T(8,128)S(1)}, ...), condition=%wide.region_8.9_spmd.clone, body=%wide.region_0.8_spmd.clone.sunk | while | flops 274503680 | bytes 7944539 | solution.py:90
  74.1 0.6 dynamic_slice.43
  75.4 0.1 fusion.37
  75.5 0.6 fusion.38
  76.7 1.9 %conditional.3 = ((f32[1,8,128]{2,1,0:T(8,128)S(1)}, f32[1,8,128]{2,1,0:T(8,128)S(1)}, f32[128,1,8,128]{0,3,2,1:T(8,128)S(1)})) conditional(s32[]{:T(128)} %convert_element_type.23, (f32[1,8,128]{2,1,0:T(8,128)S(1)}, f32[1,8,128]{2,1,0:T(8,128)S(1)}, f32[128,1,8,128]{0,3,2,1:T(8,128)S(1)}) %tuple.61, (pred[512]{0:T(512)(128)(4,1)S(1)}, ...), branch_computations={%region_4.4_spmd, %region_5.7_spmd} | conditional | flops 274467840 | bytes 7931432 | solution.py:80
  76.7 0.5 bitcast_reduce_fusion
  77.2 0.8 %fusion.5 = f32[128,1,8,128]{0,3,2,1:T(8,128)S(1)} fusion(f32[512,128,8]{1,0,2:T(8,128)S(1)} %get-tuple-element.322, f32[8,128]{1,0:T(8,128)S(1)} %bitcast.92, pred[512]{0:T(512)(128)(4,1)S(1)} %get-tuple-element.204, f32[128,1,8,128]{0,3,2,1:T(8,128)S(1)} %get-tuple-element.209, f32[128,8]{0,1:T(8,128)S(1)} %get-tuple-element.317, ...), kind=kOutput, calls=%fused_computation.8 | convolution fusion | flops 136577024 | bytes 3285508 | tf_op jit(solution)/shard_map/while/body/eval_jaxpr/cond/branch_1_fun/kgts,skd->tkgd/dot_general | solution.py:70
  78.0 0.5 fusion.4
  78.6 0.6 dynamic_slice.43
  79.8 0.1 fusion.37
  79.9 0.6 fusion.38
  81.1 1.9 %conditional.3 = ((f32[1,8,128]{2,1,0:T(8,128)S(1)}, f32[1,8,128]{2,1,0:T(8,128)S(1)}, f32[128,1,8,128]{0,3,2,1:T(8,128)S(1)})) conditional(s32[]{:T(128)} %convert_element_type.23, (f32[1,8,128]{2,1,0:T(8,128)S(1)}, f32[1,8,128]{2,1,0:T(8,128)S(1)}, f32[128,1,8,128]{0,3,2,1:T(8,128)S(1)}) %tuple.61, (pred[512]{0:T(512)(128)(4,1)S(1)}, ...), branch_computations={%region_4.4_spmd, %region_5.7_spmd} | conditional | flops 274467840 | bytes 7931432 | solution.py:80
  81.1 0.5 bitcast_reduce_fusion
  81.6 0.8 %fusion.5 = f32[128,1,8,128]{0,3,2,1:T(8,128)S(1)} fusion(f32[512,128,8]{1,0,2:T(8,128)S(1)} %get-tuple-element.322, f32[8,128]{1,0:T(8,128)S(1)} %bitcast.92, pred[512]{0:T(512)(128)(4,1)S(1)} %get-tuple-element.204, f32[128,1,8,128]{0,3,2,1:T(8,128)S(1)} %get-tuple-element.209, f32[128,8]{0,1:T(8,128)S(1)} %get-tuple-element.317, ...), kind=kOutput, calls=%fused_computation.8 | convolution fusion | flops 136577024 | bytes 3285508 | tf_op jit(solution)/shard_map/while/body/eval_jaxpr/cond/branch_1_fun/kgts,skd->tkgd/dot_general | solution.py:70
  82.4 0.5 fusion.4
  83.0 0.1 divide_convert_fusion
  83.0 0.9 %copy.32 = bf16[128,1024]{1,0:T(8,128)(2,1)} copy(bf16[128,1024]{0,1:T(8,128)(2,1)S(1)} %bitcast.94) | data formatting | bytes 524288 | tf_op jit(solution)/shard_map/reshape | solution.py:94
  (12 shorter events, 0.1 us)
Async XLA Ops:
  0.0 5.1 %copy-start = (bf16[32,512]{1,0:T(8,128)(2,1)S(1)}, bf16[32,512]{1,0:T(8,128)(2,1)}, u32[]{:S(2)}) copy-start(bf16[32,512]{1,0:T(8,128)(2,1)} %param.11) | copy-start | bytes 98308
  0.0 74.1 %copy-start.1 = (s32[8]{0:T(128)S(1)}, s32[8]{0:T(128)}, u32[]{:S(2)}) copy-start(s32[8]{0:T(128)} %param.13) | copy-start | bytes 100
  1.4 6.4 %all-to-all-start = ((bf16[4,32,128]{2,1,0:T(8,128)(2,1)}), bf16[4,32,128]{2,1,0:T(8,128)(2,1)S(1)}, u32[]{:S(2)}, u32[]{:S(2)}) async-start(bf16[4,32,128]{2,1,0:T(8,128)(2,1)} %pad_maximum_fusion), calls=%async_computation | async-start | bytes 65536 | tf_op jit(solution)/shard_map/all_to_all | solution.py:101
  7.8 35.4 %all-to-all-start.1 = ((bf16[32,4,128]{2,0,1:T(8,128)(2,1)}), bf16[32,4,128]{2,0,1:T(8,128)(2,1)S(1)}, u32[]{:S(2)}, u32[]{:S(2)}) async-start(bf16[32,4,128]{2,0,1:T(8,128)(2,1)} %copy_bitcast_fusion), calls=%async_computation.1 | async-start | bytes 65536 | tf_op jit(solution)/shard_map/all_to_all | solution.py:106
